TPU v7x, 512 devices: a whole 4x8x8 slice. The times are simulated.
512 devices in a mesh: blk: 512 (over x, z, y, core).
Axes of the slice: x: 4, y: 8, z: 8, core: 2. Of those that a mesh axis runs over, the one named last changes fastest.
Arguments:
- positive_row: float32 [256, 131072], P(None, 'blk'), may hold values from -6 to 160, as said below
- negative_row: float32 [256, 131072], P(None, 'blk'), may hold values from -5 to 5
Outputs:
- positive_out: float32 [256, 131072], P(None, 'blk')
- negative_out: float32 [256, 131072], P(None, 'blk')
Inputs may be any that keep to these rules, and one draw needn't show every extreme that they name: `positive_row`: the first 256 columns form an upper triangular block whose diagonal lies between 80 and 160.
All inputs are finite; a program needn't handle non-finite values.
Results may differ from a plain program's by a relative error of at most 0.00017.
Values sent between devices are 32-bit elements; how exact they have to be, the bound alone decides.
No kernel may reach another device: no remote copies, remote signals or barrier semaphores. Data moves between devices by JAX's collectives and lax.ppermute only.
A program may use at most 64 MiB of HBM per device.

v0:
```python
import jax
import jax.numpy as jnp
from jax import lax
from jax.experimental import pallas as pl
from jax.experimental.pallas import tpu as pltpu
from jax.sharding import PartitionSpec as P


B = 256
AXIS = "blk"

XS, ZS, YS = 4, 8, 8


def position(x, z, y, core):
    return (((x % XS) * ZS + z % ZS) * YS + y % YS) * 2 + core


TREE = (
    (
        ((0, 0, 2), (0, 0, -2), (0, 0, 4)),
        ((0, 0, -1), (0, 2, 0), (0, 2, -1)),
        ((0, 4, 0), (0, 1, 0), (0, -3, 0)),
        ((1, 0, 0), (-1, 0, 0), (2, 0, 0)),
    ),
    (
        ((2, 0, 0), (-1, 0, 0), (1, 0, 0)),
        ((0, 0, 2), (0, 0, -2), (0, 0, 4)),
        ((0, 2, 0), (0, -2, 0), (0, 4, 0)),
        ((0, 0, 1), (0, -1, 0), (0, -1, 1)),
    ),
)


def tree_rounds():
    holders = [[(0, 0, 0)], [(0, 0, 0)]]
    rounds = []
    for r in range(len(TREE[0])):
        permutes = []
        fresh = [[], []]
        for k in range(len(TREE[0][r])):
            pairs = []
            for core in range(2):
                dx, dz, dy = TREE[core][r][k]
                for x, z, y in holders[core]:
                    to = ((x + dx) % XS, (z + dz) % ZS, (y + dy) % YS)
                    fresh[core].append(to)
                    pairs.append((position(x, z, y, core), position(*to, core)))
            permutes.append(pairs)
        for core in range(2):
            holders[core] += fresh[core]
        rounds.append(permutes)
    return rounds


def halves(a):
    high = a.astype(jnp.bfloat16)
    low = (a - high.astype(jnp.float32)).astype(jnp.bfloat16)
    return high, low


def dot(a, b):
    left = jnp.concatenate([a[0], a[0], a[1]], axis=1)
    right = jnp.concatenate([b[0], b[1], b[0]], axis=0)
    return jnp.dot(left, right, preferred_element_type=jnp.float32)


def eye():
    rows = lax.broadcasted_iota(jnp.int32, (B, B), 0)
    cols = lax.broadcasted_iota(jnp.int32, (B, B), 1)
    return jnp.where(rows == cols, 1.0, 0.0).astype(jnp.float32)


def coupling_of(lead_p, lead_n, identity):
    diag = jnp.sum(lead_p * identity, axis=1, keepdims=True)
    w1 = identity - lead_p * (1.0 / diag)
    h1 = halves(w1)
    w2 = dot(h1, h1)
    m1 = lead_n + dot(halves(lead_n), h1)
    h2 = halves(w2)
    w4 = dot(h2, h2)
    m2 = m1 + dot(halves(m1), h2)
    h4 = halves(w4)
    w8 = dot(h4, h4)
    m3 = m2 + dot(halves(m2), h4)
    m4 = m3 + dot(halves(m3), halves(w8))
    diag_row = jnp.sum(lead_p * identity, axis=0, keepdims=True)
    return m4 * (1.0 / diag_row)


def root_of(gram, identity):
    e = halves(gram)
    square = dot(e, e)
    inner = 0.375 * identity + 0.3125 * gram + 0.2734375 * square
    return identity + 0.5 * gram + dot(halves(square), halves(inner))


def roots_of(k, kt, identity):
    top = root_of(dot(kt, k), identity)
    bottom = root_of(dot(k, kt), identity)
    return halves(top), halves(bottom)


def stack_kernel(p_ref, n_ref, out_ref, sems):
    copies = [
        pltpu.make_async_copy(p_ref, out_ref.at[:B, :], sems.at[0]),
        pltpu.make_async_copy(n_ref, out_ref.at[B:, :], sems.at[1]),
    ]
    for copy in copies:
        copy.start()
    for copy in copies:
        copy.wait()


def first_kernel(me_ref, own_ref, out_ref):
    @pl.when(me_ref[0] != 0)
    def _():
        out_ref[...] = jnp.zeros_like(out_ref)

    @pl.when(me_ref[0] == 0)
    def _():
        out_ref[...] = coupling_of(own_ref[:B, :], own_ref[B:, :], eye())


def second_kernel(me_ref, k_ref, own_ref, first_ref, out_ref):
    @pl.when(me_ref[0] != 1)
    def _():
        out_ref[...] = k_ref[...]

    @pl.when(me_ref[0] == 1)
    def _():
        identity = eye()
        p0, n0, p1, n1 = first_ref[:B, :], first_ref[B:, :], own_ref[:B, :], own_ref[B:, :]
        k0 = coupling_of(p0, n0, identity)
        k, kt = halves(k0), halves(k0.T)
        top, bottom = roots_of(k, kt, identity)
        lead_p = dot(top, halves(p0 - dot(kt, halves(n0))))
        lead_n = dot(bottom, halves(n1 - dot(k, halves(p1))))
        out_ref[...] = coupling_of(lead_p, lead_n, identity)


def apply_kernel(k_ref, back2_ref, back1_ref, own_ref, p_ref, n_ref):
    identity = eye()
    k0, k1 = k_ref[0], k_ref[1]
    h0, t0 = halves(k0), halves(k0.T)
    h1, t1 = halves(k1), halves(k1.T)
    top0, bottom0 = roots_of(h0, t0, identity)
    top1, bottom1 = roots_of(h1, t1, identity)
    p2, n2 = back2_ref[:B, :], back2_ref[B:, :]
    p1, n1 = back1_ref[:B, :], back1_ref[B:, :]
    p0, n0 = own_ref[:B, :], own_ref[B:, :]
    cat = lambda a, b: jnp.concatenate([a, b], axis=1)
    first_p = dot(top0, halves(cat(p2, p1) - dot(t0, halves(cat(n2, n1)))))
    first_n = dot(bottom0, halves(cat(n1, n0) - dot(h0, halves(cat(p1, p0)))))
    p_ref[...] = dot(top1, halves(first_p[:, :B] - dot(t1, halves(first_n[:, :B]))))
    n_ref[...] = dot(bottom1, halves(first_n[:, B:] - dot(h1, halves(first_p[:, B:]))))


VMEM = pl.BlockSpec(memory_space=pltpu.VMEM)
SMEM = pl.BlockSpec(memory_space=pltpu.SMEM)
ANY = pl.BlockSpec(memory_space=pl.ANY)


def resident(*arrays):
    return [pltpu.with_memory_space_constraint(a, pltpu.VMEM) for a in arrays]


def send(array, pairs):
    return lax.ppermute(array, AXIS, pairs)


def steps(positive_row, negative_row):
    me = lax.axis_index(AXIS)
    devices = lax.axis_size(AXIS)
    cores = [[i, i + 1] for i in range(0, devices, 2)]
    onward = [(i, i + 1) for i in range(1, devices - 1)]
    own = pl.pallas_call(
        stack_kernel,
        out_shape=pltpu.VMEM((2 * B, B), jnp.float32),
        in_specs=[ANY] * 2,
        out_specs=VMEM,
        scratch_shapes=[pltpu.SemaphoreType.DMA((2,))],
    )(positive_row, negative_row)
    second = send(own, [(0, 1), (1, 0)])
    back1 = send(own, onward)
    place = jnp.reshape(me, (1,)).astype(jnp.int32)
    coupling = pltpu.VMEM((B, B), jnp.float32)
    held = pl.pallas_call(
        first_kernel, out_shape=coupling, in_specs=[SMEM, VMEM], out_specs=VMEM
    )(place, *resident(own))
    held = pl.pallas_call(
        second_kernel, out_shape=coupling, in_specs=[SMEM] + [VMEM] * 3, out_specs=VMEM
    )(place, *resident(held, own, second))

    back2 = send(jnp.where(me == 0, own, back1), [(0, 2)] + onward[1:])
    back1 = jnp.where(me == 1, second, back1)
    rounds = tree_rounds()
    for permutes in rounds:
        arrived = [send(held, pairs) for pairs in permutes]
        for block in arrived:
            held = held + block

    both = lax.all_gather(held, AXIS, axis=0, axis_index_groups=cores)
    return pl.pallas_call(
        apply_kernel,
        out_shape=[jax.ShapeDtypeStruct((B, B), jnp.float32)] * 2,
        in_specs=[VMEM] * 4,
        out_specs=[VMEM] * 2,
    )(*resident(both, back2, back1, own))


def solution(mesh):
    spec = P(None, AXIS)
    return jax.shard_map(
        steps, mesh=mesh, in_specs=(spec, spec), out_specs=(spec, spec), check_vma=False
    )
```

profile of v0, /device:TPU:28, one launch (start us, length us, event | category | flops | bytes accessed | tf_op | source)
XLA Modules:
  0.0 63.5 jit_solution(11469308327556363173)
XLA Ops:
  0.6 1.0 %shard_map.41.own_ref = f32[512,256]{1,0:T(8,128)S(1)} custom-call(f32[256,256]{1,0:T(8,128)} %p_ref.1, f32[256,256]{1,0:T(8,128)} %n_ref.1), custom_call_target="tpu_custom_call" | custom-call | tf_op jit(solution)/shard_map/pallas_call | solution.py:177
  1.7 0.7 %collective-permute-start = (f32[512,256]{1,0:T(8,128)S(1)}, f32[512,256]{1,0:T(8,128)S(1)}, u32[]{:S(2)}, u32[]{:S(2)}) collective-permute-start(f32[512,256]{1,0:T(8,128)S(1)} %shard_map.41.own_ref), channel_id=1, source_target_pairs={{0,1},{1,0}} | collective-permute-start | bytes 1572872 | tf_op jit(solution)/shard_map/ppermute | solution.py:169
  2.4 0.0 collective-permute-done.first_ref
  2.5 0.7 %collective-permute-start.3 = (f32[256,256]{1,0:T(8,128)S(1)}, f32[256,256]{1,0:T(8,128)S(1)}, u32[]{:S(2)}, u32[]{:S(2)}) collective-permute-start(f32[256,256]{1,0:T(8,128)S(1)} %shard_map.43), channel_id=1, source_target_pairs={{0,8},{1,129}} | collective-permute-start | bytes 786440 | tf_op jit(solution)/shard_map/ppermute | solution.py:169
  3.2 0.7 %collective-permute-start.2 = (f32[256,256]{1,0:T(8,128)S(1)}, f32[256,256]{1,0:T(8,128)S(1)}, u32[]{:S(2)}, u32[]{:S(2)}) collective-permute-start(f32[256,256]{1,0:T(8,128)S(1)} %shard_map.43), channel_id=1, source_target_pairs={{0,12},{1,385}} | collective-permute-start | bytes 786440 | tf_op jit(solution)/shard_map/ppermute | solution.py:169
  3.8 0.7 %collective-permute-start.1 = (f32[256,256]{1,0:T(8,128)S(1)}, f32[256,256]{1,0:T(8,128)S(1)}, u32[]{:S(2)}, u32[]{:S(2)}) collective-permute-start(f32[256,256]{1,0:T(8,128)S(1)} %shard_map.43), channel_id=1, source_target_pairs={{0,4},{1,257}} | collective-permute-start | bytes 786440 | tf_op jit(solution)/shard_map/ppermute | solution.py:169
  4.5 0.0 collective-permute-done.3
  4.5 0.0 collective-permute-done.2
  4.6 0.0 collective-permute-done.1
  4.6 0.1 add_add_fusion.3
  4.6 0.7 %collective-permute-start.6 = (f32[256,256]{1,0:T(8,128)S(1)}, f32[256,256]{1,0:T(8,128)S(1)}, u32[]{:S(2)}, u32[]{:S(2)}) collective-permute-start(f32[256,256]{1,0:T(8,128)S(1)} %add_add_fusion.3), channel_id=1, source_target_pairs={{0,46},{4,34},{12,42},{8,38},{1,9},{257,265},{385,393},{129,137}} | collective-permute-start | bytes 786440 | tf_op jit(solution)/shard_map/ppermute | solution.py:169
  5.3 0.7 %collective-permute-start.5 = (f32[256,256]{1,0:T(8,128)S(1)}, f32[256,256]{1,0:T(8,128)S(1)}, u32[]{:S(2)}, u32[]{:S(2)}) collective-permute-start(f32[256,256]{1,0:T(8,128)S(1)} %add_add_fusion.3), channel_id=1, source_target_pairs={{0,32},{4,36},{12,44},{8,40},{1,13},{257,269},{385,397},{129,141}} | collective-permute-start | bytes 786440 | tf_op jit(solution)/shard_map/ppermute | solution.py:169
  6.0 0.7 %collective-permute-start.4 = (f32[256,256]{1,0:T(8,128)S(1)}, f32[256,256]{1,0:T(8,128)S(1)}, u32[]{:S(2)}, u32[]{:S(2)}) collective-permute-start(f32[256,256]{1,0:T(8,128)S(1)} %add_add_fusion.3), channel_id=1, source_target_pairs={{0,14},{4,2},{12,10},{8,6},{1,5},{257,261},{385,389},{129,133}} | collective-permute-start | bytes 786440 | tf_op jit(solution)/shard_map/ppermute | solution.py:169
  6.7 1.9 %collective-permute-start.13 = (f32[512,256]{1,0:T(8,128)S(1)}, f32[512,256]{1,0:T(8,128)S(1)}, u32[]{:S(2)}, u32[]{:S(2)}) collective-permute-start(f32[512,256]{1,0:T(8,128)S(1)} %shard_map.41.own_ref), channel_id=1, source_target_pairs={{1,2},{2,3},{3,4},{4,5},{5,6},{6,7},{7,8},{8,9},{9,10},{10,11},{11... | collective-permute-start | bytes 1572872 | tf_op jit(solution)/shard_map/ppermute | solution.py:169
  8.6 0.0 collective-permute-done.6
  8.7 0.1 add_add_fusion.2
  8.7 0.7 %collective-permute-start.9 = (f32[256,256]{1,0:T(8,128)S(1)}, f32[256,256]{1,0:T(8,128)S(1)}, u32[]{:S(2)}, u32[]{:S(2)}) collective-permute-start(f32[256,256]{1,0:T(8,128)S(1)} %add_add_fusion.2), channel_id=1, source_target_pairs={{0,80},{4,84},{12,92},{8,88},{14,94},{2,82},{10,90},{6,86},{32,112... | collective-permute-start | bytes 786440 | tf_op jit(solution)/shard_map/ppermute | solution.py:169
  9.4 0.7 %collective-permute-start.8 = (f32[256,256]{1,0:T(8,128)S(1)}, f32[256,256]{1,0:T(8,128)S(1)}, u32[]{:S(2)}, u32[]{:S(2)}) collective-permute-start(f32[256,256]{1,0:T(8,128)S(1)} %add_add_fusion.2), channel_id=1, source_target_pairs={{0,16},{4,20},{12,28},{8,24},{14,30},{2,18},{10,26},{6,22},{32,48}... | collective-permute-start | bytes 786440 | tf_op jit(solution)/shard_map/ppermute | solution.py:169
  10.1 0.7 %collective-permute-start.7 = (f32[256,256]{1,0:T(8,128)S(1)}, f32[256,256]{1,0:T(8,128)S(1)}, u32[]{:S(2)}, u32[]{:S(2)}) collective-permute-start(f32[256,256]{1,0:T(8,128)S(1)} %add_add_fusion.2), channel_id=1, source_target_pairs={{0,64},{4,68},{12,76},{8,72},{14,78},{2,66},{10,74},{6,70},{32,96}... | collective-permute-start | bytes 786440 | tf_op jit(solution)/shard_map/ppermute | solution.py:169
  10.8 0.0 collective-permute-done.7
  10.8 0.1 add_add_fusion.1
  10.9 1.3 %collective-permute-start.12 = (f32[256,256]{1,0:T(8,128)S(1)}, f32[256,256]{1,0:T(8,128)S(1)}, u32[]{:S(2)}, u32[]{:S(2)}) collective-permute-start(f32[256,256]{1,0:T(8,128)S(1)} %add_add_fusion.1), channel_id=1, source_target_pairs={{0,256},{4,260},{12,268},{8,264},{14,270},{2,258},{10,266},{6,262}... | collective-permute-start | bytes 786440 | tf_op jit(solution)/shard_map/ppermute | solution.py:169
  12.2 0.7 %collective-permute-start.11 = (f32[256,256]{1,0:T(8,128)S(1)}, f32[256,256]{1,0:T(8,128)S(1)}, u32[]{:S(2)}, u32[]{:S(2)}) collective-permute-start(f32[256,256]{1,0:T(8,128)S(1)} %add_add_fusion.1), channel_id=1, source_target_pairs={{0,384},{4,388},{12,396},{8,392},{14,398},{2,386},{10,394},{6,390}... | collective-permute-start | bytes 786440 | tf_op jit(solution)/shard_map/ppermute | solution.py:169
  12.9 0.7 %collective-permute-start.10 = (f32[256,256]{1,0:T(8,128)S(1)}, f32[256,256]{1,0:T(8,128)S(1)}, u32[]{:S(2)}, u32[]{:S(2)}) collective-permute-start(f32[256,256]{1,0:T(8,128)S(1)} %add_add_fusion.1), channel_id=1, source_target_pairs={{0,128},{4,132},{12,140},{8,136},{14,142},{2,130},{10,138},{6,134}... | collective-permute-start | bytes 786440 | tf_op jit(solution)/shard_map/ppermute | solution.py:169
  13.6 3.6 %collective-permute-done.13 = f32[512,256]{1,0:T(8,128)S(1)} collective-permute-done((f32[512,256]{1,0:T(8,128)S(1)}, f32[512,256]{1,0:T(8,128)S(1)}, u32[]{:S(2)}, u32[]{:S(2)}) %collective-permute-start.13) | collective-permute-done | bytes 524320 | tf_op jit(solution)/shard_map/ppermute | solution.py:169
  17.2 0.1 broadcast_select_fusion
  17.3 2.3 %collective-permute-start.14 = (f32[512,256]{1,0:T(8,128)S(1)}, f32[512,256]{1,0:T(8,128)S(1)}, u32[]{:S(2)}, u32[]{:S(2)}) collective-permute-start(f32[512,256]{1,0:T(8,128)S(1)} %get-tuple-element.3), channel_id=1, source_target_pairs={{0,2},{2,3},{3,4},{4,5},{5,6},{6,7},{7,8},{8,9},{9,10},{10,11},{11... | collective-permute-start | bytes 1572872 | tf_op jit(solution)/shard_map/ppermute | solution.py:169
  19.6 23.9 %collective-permute-done.12 = f32[256,256]{1,0:T(8,128)S(1)} collective-permute-done((f32[256,256]{1,0:T(8,128)S(1)}, f32[256,256]{1,0:T(8,128)S(1)}, u32[]{:S(2)}, u32[]{:S(2)}) %collective-permute-start.12) | collective-permute-done | bytes 262176 | tf_op jit(solution)/shard_map/ppermute | solution.py:169
  43.6 0.1 add_add_fusion
  43.6 11.1 %all-gather = f32[512,256]{1,0:T(8,128)S(1)} all-gather(f32[256,256]{1,0:T(8,128)S(1)} %add_add_fusion), channel_id=2, replica_groups={{0,1},{2,3},{4,5},{6,7},{8,9},{10,11},{12,13},{14,15},{16,17},{18,19},{..., dimensions={0}, use_global_device_ids=true | all-gather | bytes 786432 | tf_op jit(solution)/shard_map/all_gather | solution.py:203
  54.7 3.9 %collective-permute-done.14.back2_ref = f32[512,256]{1,0:T(8,128)S(1)} collective-permute-done((f32[512,256]{1,0:T(8,128)S(1)}, f32[512,256]{1,0:T(8,128)S(1)}, u32[]{:S(2)}, u32[]{:S(2)}) %collective-permute-start.14) | collective-permute-done | bytes 524320 | tf_op jit(solution)/shard_map/ppermute | solution.py:169
  58.6 4.9 %shard_map.44 = (f32[256,256]{1,0:T(8,128)}, f32[256,256]{1,0:T(8,128)}) custom-call(f32[2,256,256]{2,1,0:T(8,128)S(1)} %bitcast.2, f32[512,256]{1,0:T(8,128)S(1)} %collective-permute-done.14.back2_ref, f32[512,256]{1,0:T(8,128)S(1)} %get-tuple-element.2.back1_ref, f32[512,256]{1,0:T(8,128)S(1)} %shard_map.41.own_ref), custom_call_target="tpu_custom_call" | custom-call | tf_op jit(solution)/shard_map/pallas_call | solution.py:204
  (8 shorter events, 0.1 us)
Async XLA Ops:
  1.7 0.7 %collective-permute-start = (f32[512,256]{1,0:T(8,128)S(1)}, f32[512,256]{1,0:T(8,128)S(1)}, u32[]{:S(2)}, u32[]{:S(2)}) collective-permute-start(f32[512,256]{1,0:T(8,128)S(1)} %shard_map.41.own_ref), channel_id=1, source_target_pairs={{0,1},{1,0}} | collective-permute-start | bytes 1572872 | tf_op jit(solution)/shard_map/ppermute | solution.py:169
  2.5 2.1 %collective-permute-start.3 = (f32[256,256]{1,0:T(8,128)S(1)}, f32[256,256]{1,0:T(8,128)S(1)}, u32[]{:S(2)}, u32[]{:S(2)}) collective-permute-start(f32[256,256]{1,0:T(8,128)S(1)} %shard_map.43), channel_id=1, source_target_pairs={{0,8},{1,129}} | collective-permute-start | bytes 786440 | tf_op jit(solution)/shard_map/ppermute | solution.py:169
  3.2 1.4 %collective-permute-start.2 = (f32[256,256]{1,0:T(8,128)S(1)}, f32[256,256]{1,0:T(8,128)S(1)}, u32[]{:S(2)}, u32[]{:S(2)}) collective-permute-start(f32[256,256]{1,0:T(8,128)S(1)} %shard_map.43), channel_id=1, source_target_pairs={{0,12},{1,385}} | collective-permute-start | bytes 786440 | tf_op jit(solution)/shard_map/ppermute | solution.py:169
  3.8 0.7 %collective-permute-start.1 = (f32[256,256]{1,0:T(8,128)S(1)}, f32[256,256]{1,0:T(8,128)S(1)}, u32[]{:S(2)}, u32[]{:S(2)}) collective-permute-start(f32[256,256]{1,0:T(8,128)S(1)} %shard_map.43), channel_id=1, source_target_pairs={{0,4},{1,257}} | collective-permute-start | bytes 786440 | tf_op jit(solution)/shard_map/ppermute | solution.py:169
  4.6 4.0 %collective-permute-start.6 = (f32[256,256]{1,0:T(8,128)S(1)}, f32[256,256]{1,0:T(8,128)S(1)}, u32[]{:S(2)}, u32[]{:S(2)}) collective-permute-start(f32[256,256]{1,0:T(8,128)S(1)} %add_add_fusion.3), channel_id=1, source_target_pairs={{0,46},{4,34},{12,42},{8,38},{1,9},{257,265},{385,393},{129,137}} | collective-permute-start | bytes 786440 | tf_op jit(solution)/shard_map/ppermute | solution.py:169
  5.3 3.3 %collective-permute-start.5 = (f32[256,256]{1,0:T(8,128)S(1)}, f32[256,256]{1,0:T(8,128)S(1)}, u32[]{:S(2)}, u32[]{:S(2)}) collective-permute-start(f32[256,256]{1,0:T(8,128)S(1)} %add_add_fusion.3), channel_id=1, source_target_pairs={{0,32},{4,36},{12,44},{8,40},{1,13},{257,269},{385,397},{129,141}} | collective-permute-start | bytes 786440 | tf_op jit(solution)/shard_map/ppermute | solution.py:169
  6.0 2.6 %collective-permute-start.4 = (f32[256,256]{1,0:T(8,128)S(1)}, f32[256,256]{1,0:T(8,128)S(1)}, u32[]{:S(2)}, u32[]{:S(2)}) collective-permute-start(f32[256,256]{1,0:T(8,128)S(1)} %add_add_fusion.3), channel_id=1, source_target_pairs={{0,14},{4,2},{12,10},{8,6},{1,5},{257,261},{385,389},{129,133}} | collective-permute-start | bytes 786440 | tf_op jit(solution)/shard_map/ppermute | solution.py:169
  6.7 10.5 %collective-permute-start.13 = (f32[512,256]{1,0:T(8,128)S(1)}, f32[512,256]{1,0:T(8,128)S(1)}, u32[]{:S(2)}, u32[]{:S(2)}) collective-permute-start(f32[512,256]{1,0:T(8,128)S(1)} %shard_map.41.own_ref), channel_id=1, source_target_pairs={{1,2},{2,3},{3,4},{4,5},{5,6},{6,7},{7,8},{8,9},{9,10},{10,11},{11... | collective-permute-start | bytes 1572872 | tf_op jit(solution)/shard_map/ppermute | solution.py:169
  8.7 2.1 %collective-permute-start.9 = (f32[256,256]{1,0:T(8,128)S(1)}, f32[256,256]{1,0:T(8,128)S(1)}, u32[]{:S(2)}, u32[]{:S(2)}) collective-permute-start(f32[256,256]{1,0:T(8,128)S(1)} %add_add_fusion.2), channel_id=1, source_target_pairs={{0,80},{4,84},{12,92},{8,88},{14,94},{2,82},{10,90},{6,86},{32,112... | collective-permute-start | bytes 786440 | tf_op jit(solution)/shard_map/ppermute | solution.py:169
  9.4 1.4 %collective-permute-start.8 = (f32[256,256]{1,0:T(8,128)S(1)}, f32[256,256]{1,0:T(8,128)S(1)}, u32[]{:S(2)}, u32[]{:S(2)}) collective-permute-start(f32[256,256]{1,0:T(8,128)S(1)} %add_add_fusion.2), channel_id=1, source_target_pairs={{0,16},{4,20},{12,28},{8,24},{14,30},{2,18},{10,26},{6,22},{32,48}... | collective-permute-start | bytes 786440 | tf_op jit(solution)/shard_map/ppermute | solution.py:169
  10.1 0.7 %collective-permute-start.7 = (f32[256,256]{1,0:T(8,128)S(1)}, f32[256,256]{1,0:T(8,128)S(1)}, u32[]{:S(2)}, u32[]{:S(2)}) collective-permute-start(f32[256,256]{1,0:T(8,128)S(1)} %add_add_fusion.2), channel_id=1, source_target_pairs={{0,64},{4,68},{12,76},{8,72},{14,78},{2,66},{10,74},{6,70},{32,96}... | collective-permute-start | bytes 786440 | tf_op jit(solution)/shard_map/ppermute | solution.py:169
  10.9 32.7 %collective-permute-start.12 = (f32[256,256]{1,0:T(8,128)S(1)}, f32[256,256]{1,0:T(8,128)S(1)}, u32[]{:S(2)}, u32[]{:S(2)}) collective-permute-start(f32[256,256]{1,0:T(8,128)S(1)} %add_add_fusion.1), channel_id=1, source_target_pairs={{0,256},{4,260},{12,268},{8,264},{14,270},{2,258},{10,266},{6,262}... | collective-permute-start | bytes 786440 | tf_op jit(solution)/shard_map/ppermute | solution.py:169
  12.2 31.4 %collective-permute-start.11 = (f32[256,256]{1,0:T(8,128)S(1)}, f32[256,256]{1,0:T(8,128)S(1)}, u32[]{:S(2)}, u32[]{:S(2)}) collective-permute-start(f32[256,256]{1,0:T(8,128)S(1)} %add_add_fusion.1), channel_id=1, source_target_pairs={{0,384},{4,388},{12,396},{8,392},{14,398},{2,386},{10,394},{6,390}... | collective-permute-start | bytes 786440 | tf_op jit(solution)/shard_map/ppermute | solution.py:169
  12.9 30.7 %collective-permute-start.10 = (f32[256,256]{1,0:T(8,128)S(1)}, f32[256,256]{1,0:T(8,128)S(1)}, u32[]{:S(2)}, u32[]{:S(2)}) collective-permute-start(f32[256,256]{1,0:T(8,128)S(1)} %add_add_fusion.1), channel_id=1, source_target_pairs={{0,128},{4,132},{12,140},{8,136},{14,142},{2,130},{10,138},{6,134}... | collective-permute-start | bytes 786440 | tf_op jit(solution)/shard_map/ppermute | solution.py:169
  17.3 41.3 %collective-permute-start.14 = (f32[512,256]{1,0:T(8,128)S(1)}, f32[512,256]{1,0:T(8,128)S(1)}, u32[]{:S(2)}, u32[]{:S(2)}) collective-permute-start(f32[512,256]{1,0:T(8,128)S(1)} %get-tuple-element.3), channel_id=1, source_target_pairs={{0,2},{2,3},{3,4},{4,5},{5,6},{6,7},{7,8},{8,9},{9,10},{10,11},{11... | collective-permute-start | bytes 1572872 | tf_op jit(solution)/shard_map/ppermute | solution.py:169
where the time goes:
time: 63.9 us; the launch traced here: 63.5 us
  waiting for transfers between devices  31.5 us (49%)
  starting transfers between devices  13.7 us (21%)
  blocking collectives  11.1 us (17%)
  Pallas kernels  6.02 us (9%)
  between operations  0.9 us (1%)
    ppermute x15, waiting for transfers between devices, send(): return lax.ppermute(array, AXIS, pairs)  31.5 us
    ppermute x15, starting transfers between devices, send(): return lax.ppermute(array, AXIS, pairs)  13.7 us
    all_gather x1, blocking collectives, steps(): both = lax.all_gather(held, AXIS, axis=0, axis_index_groups=cores)  11.1 us
    pallas_call x1, Pallas kernels, steps(): pl.pallas_call(apply_kernel, out_shape=[jax.ShapeDtypeStruct((B, B), jnp....  4.92 us
  transfers between devices with their start and end apart: 15, of which 3 were waited for; matrix products, arithmetic and copies ran while one was open for 0% of the time, Pallas kernels for 0%

commit v1 on v0

--- a/solution.py
+++ b/solution.py
@@ -19,9 +19,9 @@
 TREE = (
     (
         ((0, 0, 2), (0, 0, -2), (0, 0, 4)),
-        ((0, 0, -1), (0, 2, 0), (0, 2, -1)),
-        ((0, 4, 0), (0, 1, 0), (0, -3, 0)),
+        ((0, 2, 0), (0, -2, 0), (0, 4, 0)),
         ((1, 0, 0), (-1, 0, 0), (2, 0, 0)),
+        ((0, 0, -1), (0, 1, 0), (0, 1, -1)),
     ),
     (
         ((2, 0, 0), (-1, 0, 0), (1, 0, 0)),
@@ -192,8 +192,8 @@
         second_kernel, out_shape=coupling, in_specs=[SMEM] + [VMEM] * 3, out_specs=VMEM
     )(place, *resident(held, own, second))
 
-    back2 = send(jnp.where(me == 0, own, back1), [(0, 2)] + onward[1:])
     back1 = jnp.where(me == 1, second, back1)
+    back2 = send(back1, onward)
     rounds = tree_rounds()
     for permutes in rounds:
         arrived = [send(held, pairs) for pairs in permutes]

time: 63.9 us -> 72.1 us (1.13)
  the two profiles are of different devices: /device:TPU:28 before, /device:TPU:2 now
where the time goes in v1:
time: 72.1 us; the launch traced here: 71.7 us
  starting transfers between devices  33.4 us (46%)
  waiting for transfers between devices  28.9 us (40%)
  Pallas kernels  6.03 us (8%)
  blocking collectives  2.18 us (3%)
  between operations  0.9 us (1%)
    ppermute x15, starting transfers between devices, send(): return lax.ppermute(array, AXIS, pairs)  33.4 us
    ppermute x15, waiting for transfers between devices, send(): return lax.ppermute(array, AXIS, pairs)  28.9 us
    pallas_call x1, Pallas kernels, steps(): pl.pallas_call(apply_kernel, out_shape=[jax.ShapeDtypeStruct((B, B), jnp....  4.92 us
    all_gather x1, blocking collectives, steps(): both = lax.all_gather(held, AXIS, axis=0, axis_index_groups=cores)  2.18 us
  transfers between devices with their start and end apart: 15, of which 4 were waited for; matrix products, arithmetic and copies ran while one was open for 0% of the time, Pallas kernels for 0%

profile of v1, /device:TPU:2, one launch (start us, length us, event | category | flops | bytes accessed | tf_op | source)
XLA Modules:
  0.0 71.7 jit_solution(7734342533544109809)
XLA Ops:
  0.6 1.0 %shard_map.41.own_ref = f32[512,256]{1,0:T(8,128)S(1)} custom-call(f32[256,256]{1,0:T(8,128)} %p_ref.1, f32[256,256]{1,0:T(8,128)} %n_ref.1), custom_call_target="tpu_custom_call" | custom-call | tf_op jit(solution)/shard_map/pallas_call | solution.py:177
  1.7 0.7 collective-permute-start
  2.5 0.7 collective-permute-start.3
  3.2 0.7 collective-permute-start.2
  3.8 0.7 collective-permute-start.1
  4.5 0.0 collective-permute-done.3
  4.5 0.0 collective-permute-done.2
  4.6 0.1 add_add_fusion.3
  4.6 0.7 collective-permute-start.6
  5.3 0.7 collective-permute-start.5
  6.0 0.7 collective-permute-start.4
  6.7 20.1 %collective-permute-start.13 = (f32[512,256]{1,0:T(8,128)S(1)}, f32[512,256]{1,0:T(8,128)S(1)}, u32[]{:S(2)}, u32[]{:S(2)}) collective-permute-start(f32[512,256]{1,0:T(8,128)S(1)} %shard_map.41.own_ref), channel_id=1, source_target_pairs={{1,2},{2,3},{3,4},{4,5},{5,6},{6,7},{7,8},{8,9},{9,10},{10,11},{11... | collective-permute-start | bytes 1572872 | tf_op jit(solution)/shard_map/ppermute | solution.py:169
  26.8 0.0 collective-permute-done.5
  26.8 0.0 collective-permute-done.4
  26.8 0.1 add_add_fusion.2
  26.9 0.7 collective-permute-start.9
  27.6 0.7 collective-permute-start.8
  28.3 1.3 %collective-permute-start.7 = (f32[256,256]{1,0:T(8,128)S(1)}, f32[256,256]{1,0:T(8,128)S(1)}, u32[]{:S(2)}, u32[]{:S(2)}) collective-permute-start(f32[256,256]{1,0:T(8,128)S(1)} %add_add_fusion.2), channel_id=1, source_target_pairs={{0,128},{4,132},{12,140},{8,136},{32,160},{36,164},{44,172},{40,16... | collective-permute-start | bytes 786440 | tf_op jit(solution)/shard_map/ppermute | solution.py:169
  29.6 0.0 collective-permute-done.9
  29.6 18.3 %collective-permute-done.7 = f32[256,256]{1,0:T(8,128)S(1)} collective-permute-done((f32[256,256]{1,0:T(8,128)S(1)}, f32[256,256]{1,0:T(8,128)S(1)}, u32[]{:S(2)}, u32[]{:S(2)}) %collective-permute-start.7) | collective-permute-done | bytes 262176 | tf_op jit(solution)/shard_map/ppermute | solution.py:169
  47.9 0.1 add_add_fusion.1
  48.0 1.3 %collective-permute-start.12 = (f32[256,256]{1,0:T(8,128)S(1)}, f32[256,256]{1,0:T(8,128)S(1)}, u32[]{:S(2)}, u32[]{:S(2)}) collective-permute-start(f32[256,256]{1,0:T(8,128)S(1)} %add_add_fusion.1), channel_id=1, source_target_pairs={{0,30},{4,18},{12,26},{8,22},{32,62},{36,50},{44,58},{40,54},{96,1... | collective-permute-start | bytes 786440 | tf_op jit(solution)/shard_map/ppermute | solution.py:169
  49.3 1.3 %collective-permute-start.11 = (f32[256,256]{1,0:T(8,128)S(1)}, f32[256,256]{1,0:T(8,128)S(1)}, u32[]{:S(2)}, u32[]{:S(2)}) collective-permute-start(f32[256,256]{1,0:T(8,128)S(1)} %add_add_fusion.1), channel_id=1, source_target_pairs={{0,16},{4,20},{12,28},{8,24},{32,48},{36,52},{44,60},{40,56},{96,1... | collective-permute-start | bytes 786440 | tf_op jit(solution)/shard_map/ppermute | solution.py:169
  50.6 1.3 %collective-permute-start.10 = (f32[256,256]{1,0:T(8,128)S(1)}, f32[256,256]{1,0:T(8,128)S(1)}, u32[]{:S(2)}, u32[]{:S(2)}) collective-permute-start(f32[256,256]{1,0:T(8,128)S(1)} %add_add_fusion.1), channel_id=1, source_target_pairs={{0,14},{4,2},{12,10},{8,6},{32,46},{36,34},{44,42},{40,38},{96,110... | collective-permute-start | bytes 786440 | tf_op jit(solution)/shard_map/ppermute | solution.py:169
  52.0 0.1 broadcast_select_fusion.back1_ref
  52.0 1.9 %collective-permute-start.14 = (f32[512,256]{1,0:T(8,128)S(1)}, f32[512,256]{1,0:T(8,128)S(1)}, u32[]{:S(2)}, u32[]{:S(2)}) collective-permute-start(f32[512,256]{1,0:T(8,128)S(1)} %broadcast_select_fusion.back1_ref), channel_id=1, source_target_pairs={{1,2},{2,3},{3,4},{4,5},{5,6},{6,7},{7,8},{8,9},{9,10},{10,11},{11... | collective-permute-start | bytes 1572872 | tf_op jit(solution)/shard_map/ppermute | solution.py:169
  54.0 0.5 collective-permute-done.11
  54.5 1.5 %collective-permute-done.10 = f32[256,256]{1,0:T(8,128)S(1)} collective-permute-done((f32[256,256]{1,0:T(8,128)S(1)}, f32[256,256]{1,0:T(8,128)S(1)}, u32[]{:S(2)}, u32[]{:S(2)}) %collective-permute-start.10) | collective-permute-done | bytes 262176 | tf_op jit(solution)/shard_map/ppermute | solution.py:169
  56.0 0.1 add_add_fusion
  56.1 2.2 %all-gather = f32[512,256]{1,0:T(8,128)S(1)} all-gather(f32[256,256]{1,0:T(8,128)S(1)} %add_add_fusion), channel_id=2, replica_groups={{0,1},{2,3},{4,5},{6,7},{8,9},{10,11},{12,13},{14,15},{16,17},{18,19},{..., dimensions={0}, use_global_device_ids=true | all-gather | bytes 786432 | tf_op jit(solution)/shard_map/all_gather | solution.py:203
  58.2 8.5 %collective-permute-done.14.back2_ref = f32[512,256]{1,0:T(8,128)S(1)} collective-permute-done((f32[512,256]{1,0:T(8,128)S(1)}, f32[512,256]{1,0:T(8,128)S(1)}, u32[]{:S(2)}, u32[]{:S(2)}) %collective-permute-start.14) | collective-permute-done | bytes 524320 | tf_op jit(solution)/shard_map/ppermute | solution.py:169
  66.7 4.9 %shard_map.44 = (f32[256,256]{1,0:T(8,128)}, f32[256,256]{1,0:T(8,128)}) custom-call(f32[2,256,256]{2,1,0:T(8,128)S(1)} %bitcast.2, f32[512,256]{1,0:T(8,128)S(1)} %collective-permute-done.14.back2_ref, f32[512,256]{1,0:T(8,128)S(1)} %broadcast_select_fusion.back1_ref, f32[512,256]{1,0:T(8,128)S(1)} %shard_map.41.own_ref), custom_call_target="tpu_custom_call" | custom-call | tf_op jit(solution)/shard_map/pallas_call | solution.py:204
  (8 shorter events, 0.1 us)
Async XLA Ops:
  1.7 0.7 %collective-permute-start = (f32[512,256]{1,0:T(8,128)S(1)}, f32[512,256]{1,0:T(8,128)S(1)}, u32[]{:S(2)}, u32[]{:S(2)}) collective-permute-start(f32[512,256]{1,0:T(8,128)S(1)} %shard_map.41.own_ref), channel_id=1, source_target_pairs={{0,1},{1,0}} | collective-permute-start | bytes 1572872 | tf_op jit(solution)/shard_map/ppermute | solution.py:169
  2.5 2.1 %collective-permute-start.3 = (f32[256,256]{1,0:T(8,128)S(1)}, f32[256,256]{1,0:T(8,128)S(1)}, u32[]{:S(2)}, u32[]{:S(2)}) collective-permute-start(f32[256,256]{1,0:T(8,128)S(1)} %shard_map.43), channel_id=1, source_target_pairs={{0,8},{1,129}} | collective-permute-start | bytes 786440 | tf_op jit(solution)/shard_map/ppermute | solution.py:169
  3.2 1.4 %collective-permute-start.2 = (f32[256,256]{1,0:T(8,128)S(1)}, f32[256,256]{1,0:T(8,128)S(1)}, u32[]{:S(2)}, u32[]{:S(2)}) collective-permute-start(f32[256,256]{1,0:T(8,128)S(1)} %shard_map.43), channel_id=1, source_target_pairs={{0,12},{1,385}} | collective-permute-start | bytes 786440 | tf_op jit(solution)/shard_map/ppermute | solution.py:169
  3.8 0.7 collective-permute-start.1
  4.6 22.2 %collective-permute-start.6 = (f32[256,256]{1,0:T(8,128)S(1)}, f32[256,256]{1,0:T(8,128)S(1)}, u32[]{:S(2)}, u32[]{:S(2)}) collective-permute-start(f32[256,256]{1,0:T(8,128)S(1)} %add_add_fusion.3), channel_id=1, source_target_pairs={{0,64},{4,68},{12,76},{8,72},{1,9},{257,265},{385,393},{129,137}} | collective-permute-start | bytes 786440 | tf_op jit(solution)/shard_map/ppermute | solution.py:169
  5.3 21.5 %collective-permute-start.5 = (f32[256,256]{1,0:T(8,128)S(1)}, f32[256,256]{1,0:T(8,128)S(1)}, u32[]{:S(2)}, u32[]{:S(2)}) collective-permute-start(f32[256,256]{1,0:T(8,128)S(1)} %add_add_fusion.3), channel_id=1, source_target_pairs={{0,96},{4,100},{12,108},{8,104},{1,13},{257,269},{385,397},{129,141}} | collective-permute-start | bytes 786440 | tf_op jit(solution)/shard_map/ppermute | solution.py:169
  6.0 20.8 %collective-permute-start.4 = (f32[256,256]{1,0:T(8,128)S(1)}, f32[256,256]{1,0:T(8,128)S(1)}, u32[]{:S(2)}, u32[]{:S(2)}) collective-permute-start(f32[256,256]{1,0:T(8,128)S(1)} %add_add_fusion.3), channel_id=1, source_target_pairs={{0,32},{4,36},{12,44},{8,40},{1,5},{257,261},{385,389},{129,133}} | collective-permute-start | bytes 786440 | tf_op jit(solution)/shard_map/ppermute | solution.py:169
  6.7 45.2 %collective-permute-start.13 = (f32[512,256]{1,0:T(8,128)S(1)}, f32[512,256]{1,0:T(8,128)S(1)}, u32[]{:S(2)}, u32[]{:S(2)}) collective-permute-start(f32[512,256]{1,0:T(8,128)S(1)} %shard_map.41.own_ref), channel_id=1, source_target_pairs={{1,2},{2,3},{3,4},{4,5},{5,6},{6,7},{7,8},{8,9},{9,10},{10,11},{11... | collective-permute-start | bytes 1572872 | tf_op jit(solution)/shard_map/ppermute | solution.py:169
  26.9 2.7 %collective-permute-start.9 = (f32[256,256]{1,0:T(8,128)S(1)}, f32[256,256]{1,0:T(8,128)S(1)}, u32[]{:S(2)}, u32[]{:S(2)}) collective-permute-start(f32[256,256]{1,0:T(8,128)S(1)} %add_add_fusion.2), channel_id=1, source_target_pairs={{0,256},{4,260},{12,268},{8,264},{32,288},{36,292},{44,300},{40,29... | collective-permute-start | bytes 786440 | tf_op jit(solution)/shard_map/ppermute | solution.py:169
  27.6 2.0 %collective-permute-start.8 = (f32[256,256]{1,0:T(8,128)S(1)}, f32[256,256]{1,0:T(8,128)S(1)}, u32[]{:S(2)}, u32[]{:S(2)}) collective-permute-start(f32[256,256]{1,0:T(8,128)S(1)} %add_add_fusion.2), channel_id=1, source_target_pairs={{0,384},{4,388},{12,396},{8,392},{32,416},{36,420},{44,428},{40,42... | collective-permute-start | bytes 786440 | tf_op jit(solution)/shard_map/ppermute | solution.py:169
  28.3 19.6 %collective-permute-start.7 = (f32[256,256]{1,0:T(8,128)S(1)}, f32[256,256]{1,0:T(8,128)S(1)}, u32[]{:S(2)}, u32[]{:S(2)}) collective-permute-start(f32[256,256]{1,0:T(8,128)S(1)} %add_add_fusion.2), channel_id=1, source_target_pairs={{0,128},{4,132},{12,140},{8,136},{32,160},{36,164},{44,172},{40,16... | collective-permute-start | bytes 786440 | tf_op jit(solution)/shard_map/ppermute | solution.py:169
  48.0 6.0 %collective-permute-start.12 = (f32[256,256]{1,0:T(8,128)S(1)}, f32[256,256]{1,0:T(8,128)S(1)}, u32[]{:S(2)}, u32[]{:S(2)}) collective-permute-start(f32[256,256]{1,0:T(8,128)S(1)} %add_add_fusion.1), channel_id=1, source_target_pairs={{0,30},{4,18},{12,26},{8,22},{32,62},{36,50},{44,58},{40,54},{96,1... | collective-permute-start | bytes 786440 | tf_op jit(solution)/shard_map/ppermute | solution.py:169
  49.3 5.2 %collective-permute-start.11 = (f32[256,256]{1,0:T(8,128)S(1)}, f32[256,256]{1,0:T(8,128)S(1)}, u32[]{:S(2)}, u32[]{:S(2)}) collective-permute-start(f32[256,256]{1,0:T(8,128)S(1)} %add_add_fusion.1), channel_id=1, source_target_pairs={{0,16},{4,20},{12,28},{8,24},{32,48},{36,52},{44,60},{40,56},{96,1... | collective-permute-start | bytes 786440 | tf_op jit(solution)/shard_map/ppermute | solution.py:169
  50.6 5.4 %collective-permute-start.10 = (f32[256,256]{1,0:T(8,128)S(1)}, f32[256,256]{1,0:T(8,128)S(1)}, u32[]{:S(2)}, u32[]{:S(2)}) collective-permute-start(f32[256,256]{1,0:T(8,128)S(1)} %add_add_fusion.1), channel_id=1, source_target_pairs={{0,14},{4,2},{12,10},{8,6},{32,46},{36,34},{44,42},{40,38},{96,110... | collective-permute-start | bytes 786440 | tf_op jit(solution)/shard_map/ppermute | solution.py:169
  52.0 14.7 %collective-permute-start.14 = (f32[512,256]{1,0:T(8,128)S(1)}, f32[512,256]{1,0:T(8,128)S(1)}, u32[]{:S(2)}, u32[]{:S(2)}) collective-permute-start(f32[512,256]{1,0:T(8,128)S(1)} %broadcast_select_fusion.back1_ref), channel_id=1, source_target_pairs={{1,2},{2,3},{3,4},{4,5},{5,6},{6,7},{7,8},{8,9},{9,10},{10,11},{11... | collective-permute-start | bytes 1572872 | tf_op jit(solution)/shard_map/ppermute | solution.py:169
